TPU v7x, 32 devices: a whole 2x2x4 slice. The times are simulated.
32 devices in a mesh: dp: 8 (over z, x), ctx: 4 (over y, core).
Axes of the slice: x: 2, y: 2, z: 4, core: 2. Of those that a mesh axis runs over, the one named last changes fastest.
Arguments:
- inputs: bfloat16 [8, 512, 5376], P('dp', 'ctx'), may hold values from -6 to 6
- q_proj: bfloat16 [8, 512, 2048], P('dp', 'ctx'), may hold values from -260 to 260
- k_proj: bfloat16 [8, 512, 1024], P('dp', 'ctx'), may hold values from -260 to 260
- v_proj: bfloat16 [8, 512, 1024], P('dp', 'ctx'), may hold values from -6 to 6
- d_attn: bfloat16 [8, 512, 2048], P('dp', 'ctx'), may hold values from -6 to 6
- positions: int32 [8, 512], P('dp', 'ctx'), may hold values from 0 to 511, as said below
- windows: int32 [8], P('dp'), may hold values from 512 to 1024
- q_gain: float32 [128], replicated, may hold values from 0.7 to 5.5
- k_gain: float32 [128], replicated, may hold values from 0.7 to 5.5
- weight: bfloat16 [5376, 4096], P('dp'), may hold values from -0.078125 to 0.078125
Outputs:
- d_inputs: bfloat16 [8, 512, 5376], P('dp', 'ctx')
- d_weight_t: float32 [4096, 5376], P('ctx', 'dp')
- d_q_gain: float32 [128], replicated
- d_k_gain: float32 [128], replicated
Inputs may be any that keep to these rules, and one draw needn't show every extreme that they name: `positions`: within each sequence a position counts the tokens since its document began: it grows by one from token to token and falls to 0 where a document begins; the first token of a sequence has position 0. Some sequence holds a single document.
All inputs are finite; a program needn't handle non-finite values.
Results may differ from a plain program's by a relative error of at most 0.029.
Values may be sent and summed in bfloat16 or wider, within the bound.
A program may use at most 128 MiB of HBM per device.

v0:
```python
import math
import jax
import jax.numpy as jnp
from jax import lax
from jax.sharding import PartitionSpec as P

REACH = 8
score_scale = 168.0 ** (-0.5)
rope_base = 10000.0
norm_eps = 1e-06


def from_behind(value, axis, steps):
    count = lax.axis_size(axis)
    initial, last = (max(0, -steps), min(count, count - steps))
    return lax.ppermute(value, axis, [(source, source + steps) for source in range(initial, last)])


def rotated_unit(projected_rows, gain_vector, token_pos, head_count):
    head_width = gain_vector.shape[0]
    rows_heads = projected_rows.reshape(projected_rows.shape[0], head_count, head_width)
    inverse = lax.rsqrt(jnp.mean(rows_heads * rows_heads, axis=-1, keepdims=True) + norm_eps)
    normed = rows_heads * inverse * gain_vector
    half_width = head_width // 2
    frequency = jnp.exp(
        jnp.arange(half_width, dtype=jnp.float32) * (-2.0 * math.log(rope_base) / head_width)
    )
    angles = token_pos.astype(jnp.float32)[:, None] * frequency[None, :]
    cosine_table = jnp.cos(angles)[:, None, :]
    sine_table = jnp.sin(angles)[:, None, :]
    first_half = normed[..., :half_width]
    second_half = normed[..., half_width:]
    return jnp.concatenate(
        [
            first_half * cosine_table - second_half * sine_table,
            second_half * cosine_table + first_half * sine_table,
        ],
        axis=-1,
    )


def shards(inputs, q_proj, k_proj, v_proj, d_attn, positions, windows, q_gain, k_gain, weight):
    tok_rows = inputs.shape[1]
    head_width = q_gain.shape[0]
    query_heads = q_proj.shape[2] // head_width
    key_heads = k_proj.shape[2] // head_width
    group_size = query_heads // key_heads
    token_pos = positions[0]
    window = windows[0]
    input_cols = lax.all_to_all(inputs, "dp", split_axis=2, concat_axis=0, tiled=True)

    def query_side(projected_rows, gain_vector):
        return rotated_unit(projected_rows, gain_vector, token_pos, query_heads)

    def key_side(projected_rows, gain_vector):
        return rotated_unit(projected_rows, gain_vector, token_pos, key_heads)

    q_full, query_back = jax.vjp(query_side, q_proj[0].astype(jnp.float32), q_gain)
    k_full, key_back = jax.vjp(key_side, k_proj[0].astype(jnp.float32), k_gain)
    query_rotated = q_full.astype(jnp.bfloat16).reshape(tok_rows, key_heads, group_size, head_width)
    key_rotated = k_full.astype(jnp.bfloat16)
    v_own = v_proj[0].reshape(tok_rows, key_heads, head_width)
    reach_count = min(REACH, lax.axis_size("ctx") - 1)
    key_blocks = [key_rotated]
    value_blocks = [v_own]
    for distance_steps in range(1, reach_count + 1):
        far_keys, far_values = from_behind((key_rotated, v_own), "ctx", distance_steps)
        key_blocks.append(far_keys)
        value_blocks.append(far_values)
    all_keys = jnp.stack(key_blocks)
    all_values = jnp.stack(value_blocks)
    block_ids = jnp.arange(reach_count + 1, dtype=jnp.int32)
    offsets = jnp.arange(tok_rows, dtype=jnp.int32)
    distance = block_ids[None, :, None] * tok_rows + offsets[:, None, None] - offsets[None, None, :]
    allowed = (distance >= 0) & (distance < window) & (distance <= token_pos[:, None, None])
    scores = (
        jnp.einsum("ahgd,bchd->hgabc", query_rotated, all_keys, preferred_element_type=jnp.float32)
        * score_scale
    )
    scores = jnp.where(allowed, scores, -jnp.inf)
    row_max = jnp.max(scores, axis=(3, 4), keepdims=True)
    exponent = jnp.exp(scores - row_max)
    probs = exponent / jnp.sum(exponent, axis=(3, 4), keepdims=True)
    head_gradient = d_attn[0].reshape(tok_rows, key_heads, group_size, head_width)
    dprobs = jnp.einsum(
        "ahgd,bchd->hgabc", head_gradient, all_values, preferred_element_type=jnp.float32
    )
    delta = jnp.sum(probs * dprobs, axis=(3, 4), keepdims=True)
    dscores = (probs * (dprobs - delta)).astype(jnp.bfloat16)
    probs_low = probs.astype(jnp.bfloat16)
    dq_rot = (
        jnp.einsum("hgabc,bchd->ahgd", dscores, all_keys, preferred_element_type=jnp.float32)
        * score_scale
    )
    dk_blocks = (
        jnp.einsum("hgabc,ahgd->bchd", dscores, query_rotated, preferred_element_type=jnp.float32)
        * score_scale
    )
    dv_blocks = jnp.einsum(
        "hgabc,ahgd->bchd", probs_low, head_gradient, preferred_element_type=jnp.float32
    )
    dk_total = dk_blocks[0]
    dv_total = dv_blocks[0]
    for distance_steps in range(1, reach_count + 1):
        back_keys, back_values = from_behind(
            (
                dk_blocks[distance_steps].astype(jnp.bfloat16),
                dv_blocks[distance_steps].astype(jnp.bfloat16),
            ),
            "ctx",
            -distance_steps,
        )
        dk_total = dk_total + back_keys.astype(jnp.float32)
        dv_total = dv_total + back_values.astype(jnp.float32)
    dq_proj, dq_gain = query_back(dq_rot.reshape(tok_rows, query_heads, head_width))
    dk_proj, dk_gain = key_back(dk_total)
    dq_gain_all, dk_gain_all = lax.psum((dq_gain, dk_gain), ("dp", "ctx"))
    dv_proj = dv_total.reshape(tok_rows, key_heads * head_width)
    d_proj = jnp.concatenate([dq_proj, dk_proj, dv_proj], axis=-1).astype(jnp.bfloat16)[None]
    gathered = lax.all_gather(d_proj, "dp", axis=0, tiled=True)
    d_cols = jnp.einsum("btp,dp->btd", gathered, weight, preferred_element_type=jnp.float32)
    d_inputs = lax.all_to_all(
        d_cols.astype(jnp.bfloat16), "dp", split_axis=0, concat_axis=2, tiled=True
    )
    d_weight_t = lax.psum_scatter(
        jnp.einsum("btp,btd->pd", gathered, input_cols, preferred_element_type=jnp.float32).astype(
            jnp.bfloat16
        ),
        "ctx",
        scatter_dimension=0,
        tiled=True,
    ).astype(jnp.float32)
    return (d_inputs, d_weight_t, dq_gain_all, dk_gain_all)


def solution(mesh):
    placed = (
        P("dp", "ctx", None),
        P("dp", "ctx", None),
        P("dp", "ctx", None),
        P("dp", "ctx", None),
        P("dp", "ctx", None),
        P("dp", "ctx"),
        P("dp"),
        P(),
        P(),
        P("dp", None),
    )
    return jax.shard_map(
        shards,
        mesh=mesh,
        in_specs=placed,
        out_specs=(P("dp", "ctx", None), P("ctx", "dp"), P(), P()),
        check_vma=False,
    )
```

profile of v0, /device:TPU:0, one launch (start us, length us, event | category | flops | bytes accessed | tf_op | source)
XLA Modules:
  0.0 321.0 jit_solution(8718791477971543858)
XLA Ops:
  11.7 5.0 %collective-permute-start.2 = (bf16[128,8,128]{2,0,1:T(8,128)(2,1)}, bf16[128,8,128]{2,0,1:T(8,128)(2,1)}, u32[]{:S(2)}, u32[]{:S(2)}) collective-permute-start(bf16[128,8,128]{2,0,1:T(8,128)(2,1)} %pad_maximum_fusion.3), channel_id=1, source_target_pairs={{0,3},{4,7},{8,11},{12,15},{16,19},{20,23},{24,27},{28,31}} | collective-permute-start | bytes 786440 | tf_op jit(solution)/shard_map/ppermute | solution.py:16
  16.7 2.0 collective-permute-start
  18.7 2.0 collective-permute-start.1
  21.7 2.0 collective-permute-start.3
  23.6 2.0 collective-permute-start.4
  28.5 1.4 reshape_squeeze.7
  31.4 1.5 collective-permute-start.5
  32.9 2.1 fusion.7
  35.9 3.9 %collective-permute-done.5 = bf16[128,8,128]{2,0,1:T(8,128)(2,1)S(1)} collective-permute-done((bf16[128,8,128]{2,0,1:T(8,128)(2,1)}, bf16[128,8,128]{2,0,1:T(8,128)(2,1)S(1)}, u32[]{:S(2)}, u32[]{:S(2)}) %collective-permute-start.5) | collective-permute-done | bytes 262176 | tf_op jit(solution)/shard_map/ppermute | solution.py:16
  39.8 2.4 fusion.2
  43.6 1.7 fusion.21
  45.2 2.2 fusion.57
  47.4 3.0 fusion.56
  50.5 1.4 copy.237
  51.9 1.4 copy.238
  58.1 1.8 multiply_add_fusion.1
  60.9 1.8 fusion.22
  69.3 1.7 collective-permute-done.8
  74.0 2.3 collective-permute-done.10
  76.3 6.4 %collective-permute-done.11 = bf16[128,8,128]{0,2,1:T(8,128)(2,1)S(1)} collective-permute-done((bf16[128,8,128]{0,2,1:T(8,128)(2,1)S(1)}, bf16[128,8,128]{0,2,1:T(8,128)(2,1)S(1)}, u32[]{:S(2)}, u32[]{:S(2)}) %collective-permute-start.11) | collective-permute-done | bytes 262176 | tf_op jit(solution)/shard_map/ppermute | solution.py:16
  85.4 6.3 %copy.211 = bf16[1,128,5376]{1,0,2:T(2,128)(2,1)S(1)} copy(bf16[1,128,5376]{2,1,0:T(8,128)(2,1)} %param.10) | data formatting | bytes 2752512 | tf_op args[0]
  92.2 30.3 %reduce = bf16[5376,128]{1,0:T(8,128)(2,1)} reduce(bf16[5376,1,128]{2,1,0:T(2,128)(2,1)S(1)} %bitcast.178, bf16[]{:T(256)} %broadcast.142), dimensions={1}, to_apply=%bitcast.157.reduce_sub_computation | reduce | bytes 2752514
  122.4 3.2 %reshape.256 = bf16[8,2,43008]{2,1,0:T(2,128)(2,1)S(1)} reshape(bf16[5376,128]{1,0:T(8,128)(2,1)} %reduce) | data formatting | bytes 2752512
  125.7 71.0 %all_to_all.36 = bf16[8,2,43008]{2,1,0:T(2,128)(2,1)} all-to-all(bf16[8,2,43008]{2,1,0:T(2,128)(2,1)S(1)} %reshape.256), channel_id=1, replica_groups=mesh['dp'=8,'ctx'=4] {'dp'}, dimensions={0} | all-to-all | bytes 2752512 | tf_op jit(solution)/shard_map/all_to_all | solution.py:50
  196.7 4.5 %reshape.257 = bf16[5376,1,128]{2,1,0:T(2,128)(2,1)S(1)} reshape(bf16[8,2,43008]{2,1,0:T(2,128)(2,1)} %all_to_all.36) | data formatting | bytes 2752512
  202.5 29.1 %all-gather.2.cloned.1.call-done = bf16[8,128,4096]{2,1,0:T(8,128)(2,1)} async-done(((bf16[1,128,4096]{2,1,0:T(8,128)(2,1)}), bf16[8,128,4096]{2,1,0:T(8,128)(2,1)}) %all-gather.2.cloned.1.call-update) | async-done | bytes 8388624 | tf_op jit(solution)/shard_map/all_gather | solution.py:120
  231.6 10.2 %bitcast_convert_fusion = bf16[4096,672]{0,1:T(8,128)(2,1)} fusion(bf16[8,128,672]{1,2,0:T(8,128)(2,1)} %bitcast.192, bf16[8,128,4096]{2,1,0:T(8,128)(2,1)} %all-gather.2.cloned.1.call-done), kind=kOutput, calls=%fused_computation | convolution fusion | flops 5639897088 | bytes 15269888 | tf_op jit(solution)/shard_map/btp,btd->pd/dot_general | solution.py:126
  241.8 11.1 %fusion.18 = bf16[8,128,672]{1,2,0:T(8,128)(2,1)} fusion(bf16[8,128,4096]{2,1,0:T(8,128)(2,1)} %all-gather.2.cloned.1.call-done, bf16[672,4096]{1,0:T(8,128)(2,1)} %param.19), kind=kOutput, calls=%fused_computation.20 | convolution fusion | flops 5637832704 | bytes 15269888 | tf_op jit(solution)/shard_map/btp,dp->btd/dot_general | solution.py:121
  252.9 3.6 %all-to-all-start = ((bf16[8,128,672]{1,2,0:T(8,128)(2,1)}), bf16[8,128,672]{1,2,0:T(8,128)(2,1)S(1)}, u32[]{:S(2)}, u32[]{:S(2)}) async-start(bf16[8,128,672]{1,2,0:T(8,128)(2,1)} %fusion.18), calls=%async_computation | async-start | bytes 2752512 | tf_op jit(solution)/shard_map/all_to_all | solution.py:122
  256.4 53.0 %all-reduce.4 = (f32[128]{0:T(128)}, f32[128]{0:T(128)}) all-reduce(f32[128]{0:T(128)S(1)} %get-tuple-element.28, f32[128]{0:T(128)S(1)} %get-tuple-element.30), channel_id=1, replica_groups=mesh['dp'=8,'ctx'=4] {'dp','ctx'}, use_global_device_ids=true, to_apply=%region_9.10 | all-reduce | flops 256 | bytes 2048 | tf_op jit(solution)/shard_map/psum | solution.py:117
  309.5 1.5 copy.212
  311.0 3.2 %convert_element_type.126 = f32[1024,672]{0,1:T(8,128)} convert(bf16[1024,672]{0,1:T(8,128)(2,1)} %reduce-scatter.2.cloned.1.call-done) | non-fusion elementwise | flops 688128 | bytes 4128768 | tf_op jit(solution)/shard_map/convert_element_type | solution.py:132
  (86 shorter events, 31.2 us)
Async XLA Ops:
  7.2 13.5 %copy-start.4 = (bf16[1,128,1024]{2,1,0:T(8,128)(2,1)S(1)}, bf16[1,128,1024]{2,1,0:T(8,128)(2,1)}, u32[]{:S(2)}) copy-start(bf16[1,128,1024]{2,1,0:T(8,128)(2,1)} %param.13) | copy-start | bytes 786436
  7.2 18.5 %copy-start.2 = (bf16[1,128,2048]{2,1,0:T(8,128)(2,1)S(1)}, bf16[1,128,2048]{2,1,0:T(8,128)(2,1)}, u32[]{:S(2)}) copy-start(bf16[1,128,2048]{2,1,0:T(8,128)(2,1)} %param.11) | copy-start | bytes 1572868
  7.2 224.4 %all-gather.2.cloned.1.call-start = ((), (), s32[]{:S(2)}) async-start(), calls=%async_computation.3 | async-start | bytes 9437184 | tf_op jit(solution)/shard_map/all_gather | solution.py:120
  8.6 17.0 %copy-start = (f32[128,8,128]{2,0,1:T(8,128)}, f32[128,8,128]{2,0,1:T(8,128)S(1)}, u32[]{:S(2)}) copy-start(f32[128,8,128]{2,0,1:T(8,128)S(1)} %copy.177) | copy-start | bytes 1572868
  10.5 15.9 %copy-start.5 = (f32[128]{0:T(128)S(1)}, f32[128]{0:T(128)}, u32[]{:S(2)}) copy-start(f32[128]{0:T(128)} %param.17) | copy-start | bytes 1540
  11.7 19.7 %collective-permute-start.2 = (bf16[128,8,128]{2,0,1:T(8,128)(2,1)}, bf16[128,8,128]{2,0,1:T(8,128)(2,1)}, u32[]{:S(2)}, u32[]{:S(2)}) collective-permute-start(bf16[128,8,128]{2,0,1:T(8,128)(2,1)} %pad_maximum_fusion.3), channel_id=1, source_target_pairs={{0,3},{4,7},{8,11},{12,15},{16,19},{20,23},{24,27},{28,31}} | collective-permute-start | bytes 786440 | tf_op jit(solution)/shard_map/ppermute | solution.py:16
  16.7 16.2 %collective-permute-start = (bf16[128,8,128]{2,0,1:T(8,128)(2,1)}, bf16[128,8,128]{2,0,1:T(8,128)(2,1)}, u32[]{:S(2)}, u32[]{:S(2)}) collective-permute-start(bf16[128,8,128]{2,0,1:T(8,128)(2,1)} %pad_maximum_fusion.3), channel_id=1, source_target_pairs={{0,1},{1,2},{2,3},{4,5},{5,6},{6,7},{8,9},{9,10},{10,11},{12,13},{... | collective-permute-start | bytes 786440 | tf_op jit(solution)/shard_map/ppermute | solution.py:16
  18.7 14.3 %collective-permute-start.1 = (bf16[128,8,128]{2,0,1:T(8,128)(2,1)}, bf16[128,8,128]{2,0,1:T(8,128)(2,1)}, u32[]{:S(2)}, u32[]{:S(2)}) collective-permute-start(bf16[128,8,128]{2,0,1:T(8,128)(2,1)} %pad_maximum_fusion.3), channel_id=1, source_target_pairs={{0,2},{1,3},{4,6},{5,7},{8,10},{9,11},{12,14},{13,15},{16,18},{17,... | collective-permute-start | bytes 786440 | tf_op jit(solution)/shard_map/ppermute | solution.py:16
  21.7 14.2 %collective-permute-start.3 = (bf16[128,8,128]{2,0,1:T(8,128)(2,1)}, bf16[128,8,128]{2,0,1:T(8,128)(2,1)}, u32[]{:S(2)}, u32[]{:S(2)}) collective-permute-start(bf16[128,8,128]{2,0,1:T(8,128)(2,1)} %copy.187), channel_id=1, source_target_pairs={{0,1},{1,2},{2,3},{4,5},{5,6},{6,7},{8,9},{9,10},{10,11},{12,13},{... | collective-permute-start | bytes 786440 | tf_op jit(solution)/shard_map/ppermute | solution.py:16
  23.6 12.3 %collective-permute-start.4 = (bf16[128,8,128]{2,0,1:T(8,128)(2,1)}, bf16[128,8,128]{2,0,1:T(8,128)(2,1)}, u32[]{:S(2)}, u32[]{:S(2)}) collective-permute-start(bf16[128,8,128]{2,0,1:T(8,128)(2,1)} %copy.187), channel_id=1, source_target_pairs={{0,2},{1,3},{4,6},{5,7},{8,10},{9,11},{12,14},{13,15},{16,18},{17,... | collective-permute-start | bytes 786440 | tf_op jit(solution)/shard_map/ppermute | solution.py:16
  26.8 4.5 %copy-start.7 = (s32[1,128]{1,0:T(1,128)S(1)}, s32[1,128]{1,0:T(1,128)}, u32[]{:S(2)}) copy-start(s32[1,128]{1,0:T(1,128)} %param.15) | copy-start | bytes 1540
  31.4 8.4 %collective-permute-start.5 = (bf16[128,8,128]{2,0,1:T(8,128)(2,1)}, bf16[128,8,128]{2,0,1:T(8,128)(2,1)S(1)}, u32[]{:S(2)}, u32[]{:S(2)}) collective-permute-start(bf16[128,8,128]{2,0,1:T(8,128)(2,1)} %copy.187), channel_id=1, source_target_pairs={{0,3},{4,7},{8,11},{12,15},{16,19},{20,23},{24,27},{28,31}} | collective-permute-start | bytes 786440 | tf_op jit(solution)/shard_map/ppermute | solution.py:16
  35.0 4.8 %copy-start.3 = (bf16[128,8,2,128,1]{0,3,2,4,1:T(8,128)(2,1)S(1)}, bf16[128,8,2,128,1]{0,3,2,4,1:T(8,128)(2,1)}, u32[]{:S(2)}) copy-start(bf16[128,8,2,128,1]{0,3,2,4,1:T(8,128)(2,1)} %copy.224) | copy-start | bytes 1572868
  54.2 13.7 %collective-permute-start.6 = (bf16[128,8,128]{2,0,1:T(8,128)(2,1)}, bf16[128,8,128]{2,0,1:T(8,128)(2,1)}, u32[]{:S(2)}, u32[]{:S(2)}) collective-permute-start(bf16[128,8,128]{2,0,1:T(8,128)(2,1)} %get-tuple-element.40), channel_id=1, source_target_pairs={{1,0},{2,1},{3,2},{5,4},{6,5},{7,6},{9,8},{10,9},{11,10},{13,12},{... | collective-permute-start | bytes 786440 | tf_op jit(solution)/shard_map/ppermute | solution.py:16
  55.5 13.8 %collective-permute-start.7 = (bf16[128,8,128]{2,0,1:T(8,128)(2,1)}, bf16[128,8,128]{2,0,1:T(8,128)(2,1)}, u32[]{:S(2)}, u32[]{:S(2)}) collective-permute-start(bf16[128,8,128]{2,0,1:T(8,128)(2,1)} %get-tuple-element.42), channel_id=1, source_target_pairs={{2,0},{3,1},{6,4},{7,5},{10,8},{11,9},{14,12},{15,13},{18,16},{19,... | collective-permute-start | bytes 786440 | tf_op jit(solution)/shard_map/ppermute | solution.py:16
  56.8 14.2 %collective-permute-start.8 = (bf16[128,8,128]{2,0,1:T(8,128)(2,1)}, bf16[128,8,128]{2,0,1:T(8,128)(2,1)}, u32[]{:S(2)}, u32[]{:S(2)}) collective-permute-start(bf16[128,8,128]{2,0,1:T(8,128)(2,1)} %get-tuple-element.41), channel_id=1, source_target_pairs={{3,0},{7,4},{11,8},{15,12},{19,16},{23,20},{27,24},{31,28}} | collective-permute-start | bytes 786440 | tf_op jit(solution)/shard_map/ppermute | solution.py:16
  62.7 9.9 %copy-start.1 = (f32[128,8,128]{2,0,1:T(8,128)S(1)}, f32[128,8,128]{2,0,1:T(8,128)}, u32[]{:S(2)}) copy-start(f32[128,8,128]{2,0,1:T(8,128)} %copy-done) | copy-start | bytes 1572868
  62.7 9.9 %copy-start.6 = (f32[128]{0:T(128)S(1)}, f32[128]{0:T(128)}, u32[]{:S(2)}) copy-start(f32[128]{0:T(128)} %param.18) | copy-start | bytes 1540
  65.2 11.1 %collective-permute-start.10 = (bf16[128,8,128]{0,2,1:T(8,128)(2,1)S(1)}, bf16[128,8,128]{0,2,1:T(8,128)(2,1)S(1)}, u32[]{:S(2)}, u32[]{:S(2)}) collective-permute-start(bf16[128,8,128]{0,2,1:T(8,128)(2,1)S(1)} %get-tuple-element.45), channel_id=1, source_target_pairs={{2,0},{3,1},{6,4},{7,5},{10,8},{11,9},{14,12},{15,13},{18,16},{19,... | collective-permute-start | bytes 786440 | tf_op jit(solution)/shard_map/ppermute | solution.py:16
  66.5 16.2 %collective-permute-start.11 = (bf16[128,8,128]{0,2,1:T(8,128)(2,1)S(1)}, bf16[128,8,128]{0,2,1:T(8,128)(2,1)S(1)}, u32[]{:S(2)}, u32[]{:S(2)}) collective-permute-start(bf16[128,8,128]{0,2,1:T(8,128)(2,1)S(1)} %get-tuple-element.44), channel_id=1, source_target_pairs={{3,0},{7,4},{11,8},{15,12},{19,16},{23,20},{27,24},{31,28}} | collective-permute-start | bytes 786440 | tf_op jit(solution)/shard_map/ppermute | solution.py:16
  67.8 14.9 %collective-permute-start.9 = (bf16[128,8,128]{0,2,1:T(8,128)(2,1)S(1)}, bf16[128,8,128]{0,2,1:T(8,128)(2,1)S(1)}, u32[]{:S(2)}, u32[]{:S(2)}) collective-permute-start(bf16[128,8,128]{0,2,1:T(8,128)(2,1)S(1)} %get-tuple-element.43), channel_id=1, source_target_pairs={{1,0},{2,1},{3,2},{5,4},{6,5},{7,6},{9,8},{10,9},{11,10},{13,12},{... | collective-permute-start | bytes 786440 | tf_op jit(solution)/shard_map/ppermute | solution.py:16
  85.1 225.9 %reduce-scatter.2.cloned.1.call-start = ((), (), s32[]{:S(2)}) async-start(), calls=%async_computation.4 | async-start | bytes 6881280 | tf_op jit(solution)/shard_map/reduce_scatter | solution.py:125
  252.9 56.6 %all-to-all-start = ((bf16[8,128,672]{1,2,0:T(8,128)(2,1)}), bf16[8,128,672]{1,2,0:T(8,128)(2,1)S(1)}, u32[]{:S(2)}, u32[]{:S(2)}) async-start(bf16[8,128,672]{1,2,0:T(8,128)(2,1)} %fusion.18), calls=%async_computation | async-start | bytes 2752512 | tf_op jit(solution)/shard_map/all_to_all | solution.py:122
Sparse Core Ops, SparseCore 0:
  85.2 146.3 all-gather.1
  241.9 51.8 reduce-scatter.1
where the time goes:
time: 322 us; the launch traced here: 321 us
  blocking collectives  124 us (39%)
  other arithmetic  49.7 us (15%)
  waiting for transfers between devices  43.6 us (14%)
  matrix products  32.5 us (10%)
  local copies, waits for them, and re-layouts  30 us (9%)
  starting transfers between devices  26 us (8%)
  between operations  15.2 us (5%)
    all_to_all x1, blocking collectives, shards(): lax.all_to_all(inputs, 'dp', split_axis=2, concat_axis=0, tiled=True)  71 us
    psum x1, blocking collectives, shards(): dq_gain_all, dk_gain_all = lax.psum((dq_gain, dk_gain), ('dp', 'ctx'))  53 us
    unnamed x2, other arithmetic  30.4 us
    all_gather x1, waiting for transfers between devices, shards(): gathered = lax.all_gather(d_proj, 'dp', axis=0, tiled=True)  29.1 us
    ppermute x12, starting transfers between devices, from_behind(): lax.ppermute(value, axis, [(source, source + steps) for source in range(i...  22.2 us
    unnamed x27, local copies, waits for them, and re-layouts  21.7 us
    ppermute x12, waiting for transfers between devices, from_behind(): lax.ppermute(value, axis, [(source, source + steps) for source in range(i...  14.4 us
    dot_general x1, matrix products, shards(): jnp.einsum('btp,dp->btd', gathered, weight, preferred_element_type=jnp.fl...  11.1 us
  transfers between devices with their start and end apart: 15, of which 6 were waited for; matrix products, arithmetic and copies ran while one was open for 24% of the time, Pallas kernels for 0%

commit v1 on v0

--- a/solution.py
+++ b/solution.py
@@ -47,7 +47,9 @@
     group_size = query_heads // key_heads
     token_pos = positions[0]
     window = windows[0]
-    input_cols = lax.all_to_all(inputs, "dp", split_axis=2, concat_axis=0, tiled=True)
+    pieces = jnp.split(inputs, lax.axis_size("dp"), axis=2)
+    incoming = lax.all_to_all(jnp.stack(pieces), "dp", 0, 0)
+    input_cols = jnp.concatenate(incoming, axis=0)
 
     def query_side(projected_rows, gain_vector):
         return rotated_unit(projected_rows, gain_vector, token_pos, query_heads)

time: 322 us -> 325 us (level)
  waiting for transfers between devices: 43.6 us -> 93.1 us
  other arithmetic: 49.7 us -> 19.2 us
  local copies, waits for them, and re-layouts: 30 us -> 16.4 us
    all_gather x1, waiting for transfers between devices: 29.1 us -> 79.6 us  [shards(): gathered = lax.all_gather(d_proj, 'dp', axis=0, tiled=True)]
    unnamed x2 -> x1, other arithmetic: 30.4 us -> 0.09 us
    unnamed x27 -> x43, local copies, waits for them, and re-layouts: 21.7 us -> 7.54 us
  transfers between devices with their start and end apart: 15 -> 15, of which waited for: 6 -> 5; matrix products, arithmetic and copies ran while one was open for 24% -> 10% of each run, Pallas kernels for 0% -> 0%
where the time goes in v1:
time: 325 us; the launch traced here: 324 us
  blocking collectives  122 us (38%)
  waiting for transfers between devices  93.1 us (29%)
  matrix products  32.1 us (10%)
  starting transfers between devices  26.3 us (8%)
  other arithmetic  19.2 us (6%)
  local copies, waits for them, and re-layouts  16.4 us (5%)
  between operations  15.3 us (5%)
    all_gather x1, waiting for transfers between devices, shards(): gathered = lax.all_gather(d_proj, 'dp', axis=0, tiled=True)  79.6 us
    all_to_all x1, blocking collectives, shards(): incoming = lax.all_to_all(jnp.stack(pieces), 'dp', 0, 0)  69.5 us
    psum x1, blocking collectives, shards(): dq_gain_all, dk_gain_all = lax.psum((dq_gain, dk_gain), ('dp', 'ctx'))  52.6 us
    ppermute x12, starting transfers between devices, from_behind(): lax.ppermute(value, axis, [(source, source + steps) for source in range(i...  22.4 us
    ppermute x12, waiting for transfers between devices, from_behind(): lax.ppermute(value, axis, [(source, source + steps) for source in range(i...  13.4 us
    dot_general x1, matrix products, shards(): jnp.einsum('btp,dp->btd', gathered, weight, preferred_element_type=jnp.fl...  10.9 us
    dot_general x1, matrix products, shards(): jnp.einsum('btp,btd->pd', gathered, input_cols, preferred_element_type=jn...  9.82 us
    unnamed x43, local copies, waits for them, and re-layouts  7.54 us
  transfers between devices with their start and end apart: 15, of which 5 were waited for; matrix products, arithmetic and copies ran while one was open for 10% of the time, Pallas kernels for 0%

profile of v1, /device:TPU:0, one launch (start us, length us, event | category | flops | bytes accessed | tf_op | source)
XLA Modules:
  0.0 324.4 jit_solution(14689094630579197068)
XLA Ops:
  11.0 5.0 %collective-permute-start.2 = (bf16[128,8,128]{2,0,1:T(8,128)(2,1)S(1)}, bf16[128,8,128]{2,0,1:T(8,128)(2,1)}, u32[]{:S(2)}, u32[]{:S(2)}) collective-permute-start(bf16[128,8,128]{2,0,1:T(8,128)(2,1)S(1)} %pad_maximum_fusion.3), channel_id=1, source_target_pairs={{0,3},{4,7},{8,11},{12,15},{16,19},{20,23},{24,27},{28,31}} | collective-permute-start | bytes 786440 | tf_op jit(solution)/shard_map/ppermute | solution.py:16
  16.0 2.0 collective-permute-start
  18.0 2.0 collective-permute-start.1
  21.0 2.0 collective-permute-start.3
  23.0 2.0 collective-permute-start.4
  28.6 1.4 reshape_squeeze.7
  31.5 1.5 collective-permute-start.5
  33.0 2.1 fusion.7
  36.1 2.8 collective-permute-done.5
  38.9 2.4 fusion.2
  41.4 1.3 fusion.4
  42.7 1.7 fusion.22
  44.4 2.2 fusion.59
  46.6 3.0 fusion.58
  49.6 1.4 copy.238
  51.0 1.4 copy.239
  54.6 1.3 collective-permute-start.7
  57.2 1.5 multiply_add_fusion.1
  59.9 1.8 fusion.23
  64.1 1.4 collective-permute-start.10
  65.5 1.3 collective-permute-start.11
  69.1 1.4 fusion.41
  72.1 3.2 collective-permute-done.10
  75.3 6.4 %collective-permute-done.11 = bf16[128,8,128]{0,2,1:T(8,128)(2,1)S(1)} collective-permute-done((bf16[128,8,128]{0,2,1:T(8,128)(2,1)S(1)}, bf16[128,8,128]{0,2,1:T(8,128)(2,1)S(1)}, u32[]{:S(2)}, u32[]{:S(2)}) %collective-permute-start.11) | collective-permute-done | bytes 262176 | tf_op jit(solution)/shard_map/ppermute | solution.py:16
  86.7 69.5 %all_to_all.23 = bf16[8,1,128,672]{2,3,1,0:T(8,128)(2,1)S(1)} all-to-all(bf16[8,1,128,672]{2,3,1,0:T(8,128)(2,1)S(1)} %bitcast_dynamic-update-slice_fusion), channel_id=1, replica_groups=mesh['dp'=8,'ctx'=4] {'dp'}, dimensions={0} | all-to-all | bytes 2752512 | tf_op jit(solution)/shard_map/all_to_all | solution.py:51
  156.2 79.6 %all-gather.2.cloned.1.call-done = bf16[8,128,4096]{2,1,0:T(8,128)(2,1)} async-done(((bf16[1,128,4096]{2,1,0:T(8,128)(2,1)}), bf16[8,128,4096]{2,1,0:T(8,128)(2,1)}) %all-gather.2.cloned.1.call-update) | async-done | bytes 8388624 | tf_op jit(solution)/shard_map/all_gather | solution.py:122
  235.9 9.8 %bitcast_convert_fusion = bf16[4096,672]{0,1:T(8,128)(2,1)} fusion(bf16[8,128,4096]{2,1,0:T(8,128)(2,1)} %all-gather.2.cloned.1.call-done, bf16[8,1,128,672]{2,3,1,0:T(8,128)(2,1)S(1)} %all_to_all.23), kind=kOutput, calls=%fused_computation | convolution fusion | flops 5639897088 | bytes 15269888 | tf_op jit(solution)/shard_map/btp,btd->pd/dot_general | solution.py:128
  245.7 10.9 %fusion.18 = bf16[8,128,672]{1,2,0:T(8,128)(2,1)} fusion(bf16[8,128,4096]{2,1,0:T(8,128)(2,1)} %all-gather.2.cloned.1.call-done, bf16[672,4096]{1,0:T(8,128)(2,1)} %param.19), kind=kOutput, calls=%fused_computation.20 | convolution fusion | flops 5637832704 | bytes 15269888 | tf_op jit(solution)/shard_map/btp,dp->btd/dot_general | solution.py:123
  256.6 3.6 %all-to-all-start = ((bf16[8,128,672]{1,2,0:T(8,128)(2,1)}), bf16[8,128,672]{1,2,0:T(8,128)(2,1)S(1)}, u32[]{:S(2)}, u32[]{:S(2)}) async-start(bf16[8,128,672]{1,2,0:T(8,128)(2,1)} %fusion.18), calls=%async_computation | async-start | bytes 2752512 | tf_op jit(solution)/shard_map/all_to_all | solution.py:124
  260.2 52.6 %all-reduce.4 = (f32[128]{0:T(128)}, f32[128]{0:T(128)}) all-reduce(f32[128]{0:T(128)S(1)} %get-tuple-element.24, f32[128]{0:T(128)S(1)} %get-tuple-element.26), channel_id=1, replica_groups=mesh['dp'=8,'ctx'=4] {'dp','ctx'}, use_global_device_ids=true, to_apply=%region_9.10 | all-reduce | flops 256 | bytes 2048 | tf_op jit(solution)/shard_map/psum | solution.py:119
  312.9 1.5 copy.214
  314.4 3.2 convert_element_type.126
  (103 shorter events, 25.9 us)
Async XLA Ops:
  7.2 228.7 %all-gather.2.cloned.1.call-start = ((), (), s32[]{:S(2)}) async-start(), calls=%async_computation.3 | async-start | bytes 9437184 | tf_op jit(solution)/shard_map/all_gather | solution.py:122
  8.4 11.6 %copy-start.7 = (bf16[1,128,1024]{2,1,0:T(8,128)(2,1)S(1)}, bf16[1,128,1024]{2,1,0:T(8,128)(2,1)}, u32[]{:S(2)}) copy-start(bf16[1,128,1024]{2,1,0:T(8,128)(2,1)} %param.13) | copy-start | bytes 786436
  8.6 11.6 %copy-start = (f32[128,8,128]{2,0,1:T(8,128)}, f32[128,8,128]{2,0,1:T(8,128)S(1)}, u32[]{:S(2)}) copy-start(f32[128,8,128]{2,0,1:T(8,128)S(1)} %copy.172) | copy-start | bytes 1572868
  9.6 15.4 %copy-start.4 = (bf16[1,128,2048]{2,1,0:T(8,128)(2,1)S(1)}, bf16[1,128,2048]{2,1,0:T(8,128)(2,1)}, u32[]{:S(2)}) copy-start(bf16[1,128,2048]{2,1,0:T(8,128)(2,1)} %param.11) | copy-start | bytes 1572868
  11.0 20.6 %collective-permute-start.2 = (bf16[128,8,128]{2,0,1:T(8,128)(2,1)S(1)}, bf16[128,8,128]{2,0,1:T(8,128)(2,1)}, u32[]{:S(2)}, u32[]{:S(2)}) collective-permute-start(bf16[128,8,128]{2,0,1:T(8,128)(2,1)S(1)} %pad_maximum_fusion.3), channel_id=1, source_target_pairs={{0,3},{4,7},{8,11},{12,15},{16,19},{20,23},{24,27},{28,31}} | collective-permute-start | bytes 786440 | tf_op jit(solution)/shard_map/ppermute | solution.py:16
  16.0 17.0 %collective-permute-start = (bf16[128,8,128]{2,0,1:T(8,128)(2,1)S(1)}, bf16[128,8,128]{2,0,1:T(8,128)(2,1)}, u32[]{:S(2)}, u32[]{:S(2)}) collective-permute-start(bf16[128,8,128]{2,0,1:T(8,128)(2,1)S(1)} %pad_maximum_fusion.3), channel_id=1, source_target_pairs={{0,1},{1,2},{2,3},{4,5},{5,6},{6,7},{8,9},{9,10},{10,11},{12,13},{... | collective-permute-start | bytes 786440 | tf_op jit(solution)/shard_map/ppermute | solution.py:16
  18.0 15.0 %collective-permute-start.1 = (bf16[128,8,128]{2,0,1:T(8,128)(2,1)S(1)}, bf16[128,8,128]{2,0,1:T(8,128)(2,1)}, u32[]{:S(2)}, u32[]{:S(2)}) collective-permute-start(bf16[128,8,128]{2,0,1:T(8,128)(2,1)S(1)} %pad_maximum_fusion.3), channel_id=1, source_target_pairs={{0,2},{1,3},{4,6},{5,7},{8,10},{9,11},{12,14},{13,15},{16,18},{17,... | collective-permute-start | bytes 786440 | tf_op jit(solution)/shard_map/ppermute | solution.py:16
  21.0 15.0 %collective-permute-start.3 = (bf16[128,8,128]{2,0,1:T(8,128)(2,1)}, bf16[128,8,128]{2,0,1:T(8,128)(2,1)}, u32[]{:S(2)}, u32[]{:S(2)}) collective-permute-start(bf16[128,8,128]{2,0,1:T(8,128)(2,1)} %copy.182), channel_id=1, source_target_pairs={{0,1},{1,2},{2,3},{4,5},{5,6},{6,7},{8,9},{9,10},{10,11},{12,13},{... | collective-permute-start | bytes 786440 | tf_op jit(solution)/shard_map/ppermute | solution.py:16
  23.0 13.1 %collective-permute-start.4 = (bf16[128,8,128]{2,0,1:T(8,128)(2,1)}, bf16[128,8,128]{2,0,1:T(8,128)(2,1)}, u32[]{:S(2)}, u32[]{:S(2)}) collective-permute-start(bf16[128,8,128]{2,0,1:T(8,128)(2,1)} %copy.182), channel_id=1, source_target_pairs={{0,2},{1,3},{4,6},{5,7},{8,10},{9,11},{12,14},{13,15},{16,18},{17,... | collective-permute-start | bytes 786440 | tf_op jit(solution)/shard_map/ppermute | solution.py:16
  25.0 0.8 copy-start.8
  27.8 3.6 %copy-start.10 = (s32[1,128]{1,0:T(1,128)S(1)}, s32[1,128]{1,0:T(1,128)}, u32[]{:S(2)}) copy-start(s32[1,128]{1,0:T(1,128)} %param.15) | copy-start | bytes 1540
  31.5 7.4 %collective-permute-start.5 = (bf16[128,8,128]{2,0,1:T(8,128)(2,1)}, bf16[128,8,128]{2,0,1:T(8,128)(2,1)S(1)}, u32[]{:S(2)}, u32[]{:S(2)}) collective-permute-start(bf16[128,8,128]{2,0,1:T(8,128)(2,1)} %copy.182), channel_id=1, source_target_pairs={{0,3},{4,7},{8,11},{12,15},{16,19},{20,23},{24,27},{28,31}} | collective-permute-start | bytes 786440 | tf_op jit(solution)/shard_map/ppermute | solution.py:16
  35.2 3.7 %copy-start.5 = (bf16[128,8,2,128,1]{0,3,2,4,1:T(8,128)(2,1)S(1)}, bf16[128,8,2,128,1]{0,3,2,4,1:T(8,128)(2,1)}, u32[]{:S(2)}) copy-start(bf16[128,8,2,128,1]{0,3,2,4,1:T(8,128)(2,1)} %copy.226) | copy-start | bytes 1572868
  41.4 1.4 copy-start.6
  52.4 4.8 %copy-start.2 = (f32[128,16,64]{2,1,0:T(8,128)S(1)}, f32[128,16,64]{2,1,0:T(8,128)}, u32[]{:S(2)}) copy-start(f32[128,16,64]{2,1,0:T(8,128)} %copy.238) | copy-start | bytes 1572868
  53.3 13.5 %collective-permute-start.6 = (bf16[128,8,128]{2,0,1:T(8,128)(2,1)}, bf16[128,8,128]{2,0,1:T(8,128)(2,1)}, u32[]{:S(2)}, u32[]{:S(2)}) collective-permute-start(bf16[128,8,128]{2,0,1:T(8,128)(2,1)} %get-tuple-element.44), channel_id=1, source_target_pairs={{1,0},{2,1},{3,2},{5,4},{6,5},{7,6},{9,8},{10,9},{11,10},{13,12},{... | collective-permute-start | bytes 786440 | tf_op jit(solution)/shard_map/ppermute | solution.py:16
  54.6 13.5 %collective-permute-start.7 = (bf16[128,8,128]{2,0,1:T(8,128)(2,1)}, bf16[128,8,128]{2,0,1:T(8,128)(2,1)}, u32[]{:S(2)}, u32[]{:S(2)}) collective-permute-start(bf16[128,8,128]{2,0,1:T(8,128)(2,1)} %get-tuple-element.46), channel_id=1, source_target_pairs={{2,0},{3,1},{6,4},{7,5},{10,8},{11,9},{14,12},{15,13},{18,16},{19,... | collective-permute-start | bytes 786440 | tf_op jit(solution)/shard_map/ppermute | solution.py:16
  55.9 13.2 %collective-permute-start.8 = (bf16[128,8,128]{2,0,1:T(8,128)(2,1)}, bf16[128,8,128]{2,0,1:T(8,128)(2,1)}, u32[]{:S(2)}, u32[]{:S(2)}) collective-permute-start(bf16[128,8,128]{2,0,1:T(8,128)(2,1)} %get-tuple-element.45), channel_id=1, source_target_pairs={{3,0},{7,4},{11,8},{15,12},{19,16},{23,20},{27,24},{31,28}} | collective-permute-start | bytes 786440 | tf_op jit(solution)/shard_map/ppermute | solution.py:16
  64.1 6.7 %copy-start.1 = (f32[128,8,128]{2,0,1:T(8,128)S(1)}, f32[128,8,128]{2,0,1:T(8,128)}, u32[]{:S(2)}) copy-start(f32[128,8,128]{2,0,1:T(8,128)} %copy-done) | copy-start | bytes 1572868
  64.1 6.7 %copy-start.9 = (f32[128]{0:T(128)S(1)}, f32[128]{0:T(128)}, u32[]{:S(2)}) copy-start(f32[128]{0:T(128)} %param.18) | copy-start | bytes 1540
  64.1 11.2 %collective-permute-start.10 = (bf16[128,8,128]{0,2,1:T(8,128)(2,1)S(1)}, bf16[128,8,128]{0,2,1:T(8,128)(2,1)S(1)}, u32[]{:S(2)}, u32[]{:S(2)}) collective-permute-start(bf16[128,8,128]{0,2,1:T(8,128)(2,1)S(1)} %get-tuple-element.49), channel_id=1, source_target_pairs={{2,0},{3,1},{6,4},{7,5},{10,8},{11,9},{14,12},{15,13},{18,16},{19,... | collective-permute-start | bytes 786440 | tf_op jit(solution)/shard_map/ppermute | solution.py:16
  65.5 16.2 %collective-permute-start.11 = (bf16[128,8,128]{0,2,1:T(8,128)(2,1)S(1)}, bf16[128,8,128]{0,2,1:T(8,128)(2,1)S(1)}, u32[]{:S(2)}, u32[]{:S(2)}) collective-permute-start(bf16[128,8,128]{0,2,1:T(8,128)(2,1)S(1)} %get-tuple-element.48), channel_id=1, source_target_pairs={{3,0},{7,4},{11,8},{15,12},{19,16},{23,20},{27,24},{31,28}} | collective-permute-start | bytes 786440 | tf_op jit(solution)/shard_map/ppermute | solution.py:16
  66.8 14.9 %collective-permute-start.9 = (bf16[128,8,128]{0,2,1:T(8,128)(2,1)S(1)}, bf16[128,8,128]{0,2,1:T(8,128)(2,1)S(1)}, u32[]{:S(2)}, u32[]{:S(2)}) collective-permute-start(bf16[128,8,128]{0,2,1:T(8,128)(2,1)S(1)} %get-tuple-element.47), channel_id=1, source_target_pairs={{1,0},{2,1},{3,2},{5,4},{6,5},{7,6},{9,8},{10,9},{11,10},{13,12},{... | collective-permute-start | bytes 786440 | tf_op jit(solution)/shard_map/ppermute | solution.py:16
  82.9 1.7 copy-start.3
  84.1 230.3 %reduce-scatter.2.cloned.1.call-start = ((), (), s32[]{:S(2)}) async-start(), calls=%async_computation.4 | async-start | bytes 6881280 | tf_op jit(solution)/shard_map/reduce_scatter | solution.py:127
  256.6 56.2 %all-to-all-start = ((bf16[8,128,672]{1,2,0:T(8,128)(2,1)}), bf16[8,128,672]{1,2,0:T(8,128)(2,1)S(1)}, u32[]{:S(2)}, u32[]{:S(2)}) async-start(bf16[8,128,672]{1,2,0:T(8,128)(2,1)} %fusion.18), calls=%async_computation | async-start | bytes 2752512 | tf_op jit(solution)/shard_map/all_to_all | solution.py:124
Sparse Core Ops, SparseCore 0:
  84.2 151.5 all-gather.1
  245.8 51.9 reduce-scatter.1
